TPU v7x, 32 devices: a whole 2x2x4 slice. The times are simulated.
32 devices in a mesh: agent: 8 (over y, x, core), res: 4 (over z).
Axes of the slice: x: 2, y: 2, z: 4, core: 2. Of those that a mesh axis runs over, the one named last changes fastest.
Arguments:
- linear_cost: float32 [2048, 2048], P('agent', 'res'), may hold values from -6 to 6
- agent_type: int32 [2048], P('agent'), may hold values from 0 to 3, as said below
- block_mask: int32 [2048, 16], P('agent', 'res'), may hold values 0 or 1
- inverses: bfloat16 [4, 2048, 2048], P(None, 'res'), as said below
- cost_weight: float32 [2048], P('res'), may hold values from 0.5 to 8
- target: float32 [2048], P('res'), may hold values from -6 to 6
Outputs:
- usage: float32 [2048, 2048], P('agent', 'res')
- shared: float32 [2048], P('res')
- prices: float32 [2048], P('res')
- primal_norm: float32 [5], replicated
- dual_norm: float32 [5], replicated
Inputs may be any that keep to these rules, and one draw needn't show every extreme that they name: Each inverses[k] is exactly symmetric: inverses[k, i, j] equals inverses[k, j, i]. `agent_type`: each aligned block of 256 agents (the agents held by one device along the agent axis) holds exactly 64 agents of each type, in no particular order.
All inputs are finite; a program needn't handle non-finite values. No bound on the sum of `block_mask` on one device may be relied on, other than what follows from the above.
Results may differ from a plain program's by a relative error of at most 0.0039.
Values may be sent and summed in bfloat16 or wider, within the bound.
No kernel may reach another device: no remote copies, remote signals or barrier semaphores. Data moves between devices by JAX's collectives and lax.ppermute only.
A program may use at most 64 MiB of HBM per device.

v0:
```python
import jax
import jax.numpy as jnp
from jax import lax
from jax.sharding import PartitionSpec as P

BLK = 128
ITERS = 5
penalty = 1.0
eps = 1e-06


def on_device(linear_cost, agent_type, block_mask, inverses, cost_weight, target):
    local_agents, local_width = linear_cost.shape
    type_count = inverses.shape[0]
    group_rows = local_agents // type_count
    count = local_agents * lax.axis_size("agent")
    block_count = block_mask.shape[1]
    order = jnp.argsort(agent_type, stable=True)
    restore = jnp.argsort(order, stable=True)
    expand = jnp.broadcast_to(
        block_mask.astype(jnp.float32)[:, :, None], (local_agents, block_count, BLK)
    ).reshape(local_agents, local_width)
    usage = jnp.zeros(linear_cost.shape, jnp.float32)
    mean_usage = jnp.zeros((local_width,), jnp.float32)
    shared = jnp.zeros((local_width,), jnp.float32)
    prices = jnp.zeros((local_width,), jnp.float32)
    primal_list = []
    dual_list = []
    for iteration in range(ITERS):
        rhs = (penalty * (usage - mean_usage + shared - prices) - linear_cost).astype(jnp.bfloat16)
        grouped = rhs[order].reshape(type_count, group_rows, local_width)
        product = jnp.einsum(
            "tas,tws->taw",
            lax.all_gather(grouped, "res", axis=2, tiled=True),
            inverses,
            preferred_element_type=jnp.float32,
        )
        new_usage = product.reshape(local_agents, local_width)[restore]
        new_usage = new_usage * expand
        change_local = penalty * penalty * jnp.sum((new_usage - usage) ** 2)
        usage = new_usage
        column_sum = jnp.sum(usage, axis=0)
        usage_sum = lax.psum(column_sum, "agent")
        dual2 = lax.psum(change_local, ("agent", "res"))
        mean_usage = usage_sum / count
        shared = (cost_weight * target + penalty * (prices + mean_usage)) / (cost_weight + penalty)
        prices = prices + mean_usage - shared
        primal2 = lax.psum(count * jnp.sum((mean_usage - shared) ** 2), "res")
        primal_list.append(jnp.sqrt(primal2 + eps))
        dual_list.append(jnp.sqrt(dual2 + eps))
    primal_norm = jnp.stack(primal_list)
    dual_norm = jnp.stack(dual_list)
    return (usage, shared, prices, primal_norm, dual_norm)


def solution(mesh):
    placed = (
        P("agent", "res"),
        P("agent"),
        P("agent", "res"),
        P(None, "res", None),
        P("res"),
        P("res"),
    )
    return jax.shard_map(
        on_device,
        mesh=mesh,
        in_specs=placed,
        out_specs=(P("agent", "res"), P("res"), P("res"), P(), P()),
        check_vma=False,
    )
```

profile of v0, /device:TPU:12, one launch (start us, length us, event | category | flops | bytes accessed | tf_op | source)
XLA Modules:
  0.0 334.9 jit_solution(6932095263842248031)
XLA Ops:
  7.2 3.8 %sort.31 = (s32[256]{0:T(256)}, s32[256]{0:T(256)S(1)}) sort(s32[256]{0:T(256)} %param.7, s32[256]{0:T(256)S(1)} %iota.7), dimensions={0}, to_apply=%region_0.0 | sort | flops 2048 | bytes 4096 | tf_op jit(solution)/shard_map/jit(argsort)/sort | solution.py:18
  11.1 1.1 subtract_convert_fusion.4
  12.2 1.9 gather_fusion
  14.1 3.2 sort.32
  17.3 0.7 convert_element_type.19
  18.0 0.1 copy.11
  18.2 25.1 %all-gather.6.cloned.1.call-done = bf16[4,64,2048]{2,1,0:T(8,128)(2,1)} async-done(((bf16[4,64,512]{2,1,0:T(8,128)(2,1)}), bf16[4,64,2048]{2,1,0:T(8,128)(2,1)}) %all-gather.6.cloned.1.call-update) | async-done | bytes 1048592 | tf_op jit(solution)/shard_map/all_gather | solution.py:34
  43.3 6.4 %fusion.13 = f32[4,64,512]{2,1,0:T(8,128)S(1)} fusion(bf16[4,64,2048]{2,1,0:T(8,128)(2,1)} %all-gather.6.cloned.1.call-done, bf16[4,512,2048]{2,1,0:T(8,128)(2,1)} %param.9), kind=kOutput, calls=%fused_computation.56 | convolution fusion | flops 536870912 | bytes 9961472 | tf_op jit(solution)/shard_map/tas,tws->taw/dot_general | solution.py:32
  49.7 1.0 gather_fusion.1
  50.7 0.3 broadcast_in_dim.11
  51.0 0.1 fusion.12
  51.1 11.9 %psum.105 = f32[512]{0:T(512)S(1)} all-reduce(f32[512]{0:T(512)S(1)} %get-tuple-element.44), channel_id=1, replica_groups=mesh['agent'=8,'res'=4] {'agent'}, use_global_device_ids=true, to_apply=%region_3.4 | all-reduce | flops 512 | bytes 4096 | tf_op jit(solution)/shard_map/psum | solution.py:43
  63.0 0.6 multiply_reduce_fusion.9
  63.6 0.1 subtract_convert_fusion.3
  63.7 1.9 gather_fusion.2
  65.7 27.5 %all-gather.8.cloned.1.call-done = bf16[4,64,2048]{2,1,0:T(8,128)(2,1)} async-done(((bf16[4,64,512]{2,1,0:T(8,128)(2,1)}), bf16[4,64,2048]{2,1,0:T(8,128)(2,1)}) %all-gather.8.cloned.1.call-update) | async-done | bytes 1048592 | tf_op jit(solution)/shard_map/all_gather | solution.py:34
  93.1 6.4 %fusion.14 = f32[4,64,512]{2,1,0:T(8,128)S(1)} fusion(bf16[4,64,2048]{2,1,0:T(8,128)(2,1)} %all-gather.8.cloned.1.call-done, bf16[4,512,2048]{2,1,0:T(8,128)(2,1)} %param.9), kind=kOutput, calls=%fused_computation.57 | convolution fusion | flops 536870912 | bytes 9961472 | tf_op jit(solution)/shard_map/tas,tws->taw/dot_general | solution.py:32
  99.5 1.0 gather_fusion.3
  100.6 11.9 %psum.106 = f32[512]{0:T(512)S(1)} all-reduce(f32[512]{0:T(512)S(1)} %get-tuple-element.42), channel_id=1, replica_groups=mesh['agent'=8,'res'=4] {'agent'}, use_global_device_ids=true, to_apply=%region_5.6 | all-reduce | flops 512 | bytes 4096 | tf_op jit(solution)/shard_map/psum | solution.py:43
  112.5 0.6 multiply_reduce_fusion.8
  113.1 0.1 subtract_convert_fusion.2
  113.2 1.9 gather_fusion.4
  115.1 27.5 %all-gather.10.cloned.1.call-done = bf16[4,64,2048]{2,1,0:T(8,128)(2,1)} async-done(((bf16[4,64,512]{2,1,0:T(8,128)(2,1)}), bf16[4,64,2048]{2,1,0:T(8,128)(2,1)}) %all-gather.10.cloned.1.call-update) | async-done | bytes 1048592 | tf_op jit(solution)/shard_map/all_gather | solution.py:34
  142.6 6.4 %fusion.15 = f32[4,64,512]{2,1,0:T(8,128)S(1)} fusion(bf16[4,64,2048]{2,1,0:T(8,128)(2,1)} %all-gather.10.cloned.1.call-done, bf16[4,512,2048]{2,1,0:T(8,128)(2,1)} %param.9), kind=kOutput, calls=%fused_computation.58 | convolution fusion | flops 536870912 | bytes 9961472 | tf_op jit(solution)/shard_map/tas,tws->taw/dot_general | solution.py:32
  148.9 1.0 gather_fusion.5
  150.0 12.1 %psum.107 = f32[512]{0:T(512)S(1)} all-reduce(f32[512]{0:T(512)S(1)} %get-tuple-element.40), channel_id=1, replica_groups=mesh['agent'=8,'res'=4] {'agent'}, use_global_device_ids=true, to_apply=%region_7.8 | all-reduce | flops 512 | bytes 4096 | tf_op jit(solution)/shard_map/psum | solution.py:43
  162.1 0.6 multiply_reduce_fusion.7
  162.7 0.1 subtract_convert_fusion.1
  162.8 1.9 gather_fusion.6
  164.8 27.4 %all-gather.12.cloned.1.call-done = bf16[4,64,2048]{2,1,0:T(8,128)(2,1)} async-done(((bf16[4,64,512]{2,1,0:T(8,128)(2,1)}), bf16[4,64,2048]{2,1,0:T(8,128)(2,1)}) %all-gather.12.cloned.1.call-update) | async-done | bytes 1048592 | tf_op jit(solution)/shard_map/all_gather | solution.py:34
  192.2 6.4 %fusion.16 = f32[4,64,512]{2,1,0:T(8,128)S(1)} fusion(bf16[4,64,2048]{2,1,0:T(8,128)(2,1)} %all-gather.12.cloned.1.call-done, bf16[4,512,2048]{2,1,0:T(8,128)(2,1)} %param.9), kind=kOutput, calls=%fused_computation.59 | convolution fusion | flops 536870912 | bytes 9961472 | tf_op jit(solution)/shard_map/tas,tws->taw/dot_general | solution.py:32
  198.6 1.8 gather_fusion.7
  200.4 1.2 fusion.9
  201.5 11.9 %psum.108 = f32[512]{0:T(512)S(1)} all-reduce(f32[512]{0:T(512)S(1)} %get-tuple-element.38), channel_id=1, replica_groups=mesh['agent'=8,'res'=4] {'agent'}, use_global_device_ids=true, to_apply=%region_9.10 | all-reduce | flops 512 | bytes 4096 | tf_op jit(solution)/shard_map/psum | solution.py:43
  213.4 0.6 multiply_reduce_fusion.6
  214.0 0.1 subtract_convert_fusion
  214.1 1.9 gather_fusion.8
  218.6 24.9 %all-gather.14.cloned.1.call-done = bf16[4,64,2048]{2,1,0:T(8,128)(2,1)} async-done(((bf16[4,64,512]{2,1,0:T(8,128)(2,1)}), bf16[4,64,2048]{2,1,0:T(8,128)(2,1)}) %all-gather.14.cloned.1.call-update) | async-done | bytes 1048592 | tf_op jit(solution)/shard_map/all_gather | solution.py:34
  243.5 6.4 %fusion.17 = f32[4,64,512]{2,1,0:T(8,128)S(1)} fusion(bf16[4,64,2048]{2,1,0:T(8,128)(2,1)} %all-gather.14.cloned.1.call-done, bf16[4,512,2048]{2,1,0:T(8,128)(2,1)} %param.9), kind=kOutput, calls=%fused_computation.60 | convolution fusion | flops 536870912 | bytes 9961472 | tf_op jit(solution)/shard_map/tas,tws->taw/dot_general | solution.py:32
  249.9 1.8 gather_fusion.9
  251.7 2.8 multiply_reduce_fusion
  254.5 11.9 %psum.109 = f32[512]{0:T(512)S(1)} all-reduce(f32[512]{0:T(512)S(1)} %get-tuple-element.14), channel_id=1, replica_groups=mesh['agent'=8,'res'=4] {'agent'}, use_global_device_ids=true, to_apply=%region_11.12 | all-reduce | flops 512 | bytes 4096 | tf_op jit(solution)/shard_map/psum | solution.py:43
  266.3 0.6 multiply_reduce_fusion.5
  267.6 0.6 fusion
  268.2 9.8 %all-reduce.1 = (f32[]{:T(128)}, f32[]{:T(128)}, f32[]{:T(128)}, f32[]{:T(128)}, f32[]{:T(128)}) all-reduce(f32[]{:T(128)S(6)} %mul.99, f32[]{:T(128)S(6)} %mul.100, f32[]{:T(128)S(6)} %mul.101, f32[]{:T(128)S(6)} %mul.102, f32[]{:T(128)S(6)} %mul.103), channel_id=1, replica_groups=mesh['agent'=8,'res'=4] {'res'}, use_global_device_ids=true, to_apply=%region_13.14 | all-reduce | flops 5 | bytes 40 | tf_op jit(solution)/shard_map/psum | solution.py:48
  281.3 42.5 %all-reduce = (f32[]{:T(128)}, f32[]{:T(128)}, f32[]{:T(128)}, f32[]{:T(128)}, f32[]{:T(128)}) all-reduce(f32[]{:T(128)} %get-tuple-element.13, f32[]{:T(128)} %get-tuple-element.12, f32[]{:T(128)} %get-tuple-element.11, f32[]{:T(128)} %get-tuple-element.10, f32[]{:T(128)} %get-tuple-element.9), channel_id=1, replica_groups=mesh['agent'=8,'res'=4] {'agent','res'}, use_global_device_ids=true, to_apply=%region_23.24 | all-reduce | flops 5 | bytes 40 | tf_op jit(solution)/shard_map/psum | solution.py:44
  327.2 0.6 stack.41
  327.8 0.6 stack.47
  (29 shorter events, 0.6 us)
Async XLA Ops:
  7.2 36.1 %all-gather.6.cloned.1.call-start = ((), (), s32[]{:S(2)}) async-start(), calls=%async_computation | async-start | bytes 1310720 | tf_op jit(solution)/shard_map/all_gather | solution.py:34
  14.0 79.1 %all-gather.8.cloned.1.call-start = ((), (), s32[]{:S(2)}) async-start(), calls=%async_computation.1 | async-start | bytes 1310720 | tf_op jit(solution)/shard_map/all_gather | solution.py:34
  18.1 44.9 %copy-start.1 = (f32[512]{0:T(512)S(1)}, f32[512]{0:T(512)}, u32[]{:S(2)}) copy-start(f32[512]{0:T(512)} %param.10) | copy-start | bytes 6148
  18.1 44.9 %copy-start.3 = (f32[512]{0:T(512)S(1)}, f32[512]{0:T(512)}, u32[]{:S(2)}) copy-start(f32[512]{0:T(512)} %param.11) | copy-start | bytes 6148
  18.1 45.5 %copy-start = (f32[256,512]{1,0:T(8,128)S(1)}, f32[256,512]{1,0:T(8,128)}, u32[]{:S(2)}) copy-start(f32[256,512]{1,0:T(8,128)} %param.6) | copy-start | bytes 1572868
  65.6 77.0 %all-gather.10.cloned.1.call-start = ((), (), s32[]{:S(2)}) async-start(), calls=%async_computation.2 | async-start | bytes 1310720 | tf_op jit(solution)/shard_map/all_gather | solution.py:34
  115.1 77.2 %all-gather.12.cloned.1.call-start = ((), (), s32[]{:S(2)}) async-start(), calls=%async_computation.3 | async-start | bytes 1310720 | tf_op jit(solution)/shard_map/all_gather | solution.py:34
  164.7 78.8 %all-gather.14.cloned.1.call-start = ((), (), s32[]{:S(2)}) async-start(), calls=%async_computation.4 | async-start | bytes 1310720 | tf_op jit(solution)/shard_map/all_gather | solution.py:34
  267.0 61.4 %copy-start.2 = (f32[512]{0:T(512)}, f32[512]{0:T(512)S(1)}, u32[]{:S(2)}) copy-start(f32[512]{0:T(512)S(1)} %get-tuple-element.26) | copy-start | bytes 6148
Sparse Core Ops, SparseCore 0:
  14.2 29.0 all-gather.5
  65.7 27.3 all-gather.7
  115.2 27.3 all-gather.9
  164.8 27.3 all-gather.11
  216.1 27.3 all-gather.13
where the time goes:
time: 336 us; the launch traced here: 335 us
  waiting for transfers between devices  132 us (39%)
  blocking collectives  112 us (33%)
  matrix products  31.9 us (9%)
  between operations  23.8 us (7%)
  local copies, waits for them, and re-layouts  17.4 us (5%)
  other arithmetic  17.3 us (5%)
    all_gather x5, waiting for transfers between devices, on_device(): lax.all_gather(grouped, 'res', axis=2, tiled=True)  132 us
    psum x5, blocking collectives, on_device(): usage_sum = lax.psum(column_sum, 'agent')  59.6 us
    psum x1, blocking collectives, on_device(): dual2 = lax.psum(change_local, ('agent', 'res'))  42.5 us
    dot_general x5, matrix products, on_device(): jnp.einsum('tas,tws->taw', lax.all_gather(grouped, 'res', axis=2, tiled=T...  31.9 us
    psum x1, blocking collectives, on_device(): primal2 = lax.psum(count * jnp.sum((mean_usage - shared) ** 2), 'res')  9.78 us
    gather x5, local copies, waits for them, and re-layouts, on_device(): grouped = rhs[order].reshape(type_count, group_rows, local_width)  9.27 us
  transfers between devices with their start and end apart: 5, of which 5 were waited for; matrix products, arithmetic and copies ran while one was open for 1% of the time, Pallas kernels for 0%

commit v1 on v0

--- a/solution.py
+++ b/solution.py
@@ -29,12 +29,22 @@
     for iteration in range(ITERS):
         rhs = (penalty * (usage - mean_usage + shared - prices) - linear_cost).astype(jnp.bfloat16)
         grouped = rhs[order].reshape(type_count, group_rows, local_width)
-        product = jnp.einsum(
-            "tas,tws->taw",
-            lax.all_gather(grouped, "res", axis=2, tiled=True),
-            inverses,
-            preferred_element_type=jnp.float32,
-        )
+        size, place, extent = (lax.axis_size("res"), lax.axis_index("res"), grouped.shape[2])
+        right = [(i, (i + 1) % size) for i in range(size)]
+        held, so_far = (grouped, None)
+        for turn in range(size):
+            upcoming = lax.ppermute(held, "res", right) if turn < size - 1 else None
+            update = jnp.einsum(
+                "tas,tws->taw",
+                held,
+                lax.dynamic_slice_in_dim(
+                    inverses, (place - turn) % size * extent, held.shape[2], axis=2
+                ),
+                preferred_element_type=jnp.float32,
+            )
+            so_far = update if so_far is None else so_far + update
+            held = upcoming
+        product = so_far
         new_usage = product.reshape(local_agents, local_width)[restore]
         new_usage = new_usage * expand
         change_local = penalty * penalty * jnp.sum((new_usage - usage) ** 2)

time: 336 us -> 295 us (0.88); the launches traced: 335 us -> 290 us
  waiting for transfers between devices: 132 us -> 86.3 us
  matrix products: 31.9 us -> 47.1 us
  between operations: 23.8 us -> 10.8 us
  starting transfers between devices: 0.21 us -> 4.4 us
  local copies, waits for them, and re-layouts: 17.4 us -> 13.9 us
    all_gather x5 -> x0, waiting for transfers between devices: 132 us -> none  [on_device(): lax.all_gather(grouped, 'res', axis=2, tiled=True)]
    ppermute x0 -> x15, waiting for transfers between devices: none -> 86.3 us  [on_device(): upcoming = lax.ppermute(held, 'res', right) if turn < size - 1 else None]
    dot_general x5 -> x20, matrix products: 31.9 us -> 47.1 us  [on_device(): jnp.einsum('tas,tws->taw', held, lax.dynamic_slice_in_dim(inverses, (plac...]
    ppermute x0 -> x15, starting transfers between devices: none -> 4.4 us  [on_device(): upcoming = lax.ppermute(held, 'res', right) if turn < size - 1 else None]
    gather x5, local copies, waits for them, and re-layouts: 9.27 us -> 5.77 us  [on_device(): grouped = rhs[order].reshape(type_count, group_rows, local_width)]
  transfers between devices with their start and end apart: 5 -> 15, of which waited for: 5 -> 15; matrix products, arithmetic and copies ran while one was open for 1% -> 14% of each run, Pallas kernels for 0% -> 0%
where the time goes in v1:
time: 295 us; the launch traced here: 290 us
  blocking collectives  111 us (38%)
  waiting for transfers between devices  86.3 us (29%)
  matrix products  47.1 us (16%)
  other arithmetic  17.3 us (6%)
  local copies, waits for them, and re-layouts  13.9 us (5%)
  between operations  10.8 us (4%)
  starting transfers between devices  4.4 us (1%)
    ppermute x15, waiting for transfers between devices, on_device(): upcoming = lax.ppermute(held, 'res', right) if turn < size - 1 else None  86.3 us
    psum x5, blocking collectives, on_device(): usage_sum = lax.psum(column_sum, 'agent')  59 us
    dot_general x20, matrix products, on_device(): jnp.einsum('tas,tws->taw', held, lax.dynamic_slice_in_dim(inverses, (plac...  47.1 us
    psum x1, blocking collectives, on_device(): dual2 = lax.psum(change_local, ('agent', 'res'))  43 us
    psum x1, blocking collectives, on_device(): primal2 = lax.psum(count * jnp.sum((mean_usage - shared) ** 2), 'res')  8.66 us
    gather x5, local copies, waits for them, and re-layouts, on_device(): new_usage = product.reshape(local_agents, local_width)[restore]  6.44 us
  transfers between devices with their start and end apart: 15, of which 15 were waited for; matrix products, arithmetic and copies ran while one was open for 14% of the time, Pallas kernels for 0%

profile of v1, /device:TPU:12, one launch (start us, length us, event | category | flops | bytes accessed | tf_op | source)
XLA Modules:
  0.0 290.5 jit_solution(1435112417140896543)
XLA Ops:
  0.6 3.8 %sort.31 = (s32[256]{0:T(256)}, s32[256]{0:T(256)S(1)}) sort(s32[256]{0:T(256)} %param.7, s32[256]{0:T(256)S(1)} %iota.7), dimensions={0}, to_apply=%region_0.0 | sort | flops 2048 | bytes 4096 | tf_op jit(solution)/shard_map/jit(argsort)/sort | solution.py:18
  6.7 1.6 collective-permute-start
  8.4 3.2 %sort.32 = (s32[256]{0:T(256)}, s32[256]{0:T(256)S(1)}) sort(s32[256]{0:T(256)S(1)} %get-tuple-element.7, s32[256]{0:T(256)S(1)} %iota.8), dimensions={0}, to_apply=%region_1.2 | sort | flops 2048 | bytes 4096 | tf_op jit(solution)/shard_map/jit(argsort)/sort | solution.py:19
  11.5 3.3 %collective-permute-done = bf16[4,64,512]{2,1,0:T(8,128)(2,1)S(1)} collective-permute-done((bf16[4,64,512]{2,1,0:T(8,128)(2,1)S(1)}, bf16[4,64,512]{2,1,0:T(8,128)(2,1)S(1)}, u32[]{:S(2)}, u32[]{:S(2)}) %collective-permute-start) | collective-permute-done | bytes 262176 | tf_op jit(solution)/shard_map/ppermute | solution.py:36
  17.3 2.3 fusion.23
  19.6 3.0 %collective-permute-done.1 = bf16[4,64,512]{2,1,0:T(8,128)(2,1)S(1)} collective-permute-done((bf16[4,64,512]{2,1,0:T(8,128)(2,1)S(1)}, bf16[4,64,512]{2,1,0:T(8,128)(2,1)S(1)}, u32[]{:S(2)}, u32[]{:S(2)}) %collective-permute-start.1) | collective-permute-done | bytes 262176 | tf_op jit(solution)/shard_map/ppermute | solution.py:36
  23.6 2.3 convolution_add_fusion.14
  25.9 2.3 convolution_add_fusion.13
  28.3 2.6 collective-permute-done.2
  30.8 2.3 convolution_add_fusion.12
  34.6 11.8 %psum.105 = f32[512]{0:T(512)S(1)} all-reduce(f32[512]{0:T(512)S(1)} %get-tuple-element.44), channel_id=1, replica_groups=mesh['agent'=8,'res'=4] {'agent'}, use_global_device_ids=true, to_apply=%region_3.4 | all-reduce | flops 512 | bytes 4096 | tf_op jit(solution)/shard_map/psum | solution.py:53
  48.4 9.8 %collective-permute-done.3 = bf16[4,64,512]{2,1,0:T(8,128)(2,1)S(1)} collective-permute-done((bf16[4,64,512]{2,1,0:T(8,128)(2,1)S(1)}, bf16[4,64,512]{2,1,0:T(8,128)(2,1)S(1)}, u32[]{:S(2)}, u32[]{:S(2)}) %collective-permute-start.3) | collective-permute-done | bytes 262176 | tf_op jit(solution)/shard_map/ppermute | solution.py:36
  58.2 2.3 fusion.21
  60.6 6.6 %collective-permute-done.4 = bf16[4,64,512]{2,1,0:T(8,128)(2,1)S(1)} collective-permute-done((bf16[4,64,512]{2,1,0:T(8,128)(2,1)S(1)}, bf16[4,64,512]{2,1,0:T(8,128)(2,1)S(1)}, u32[]{:S(2)}, u32[]{:S(2)}) %collective-permute-start.4) | collective-permute-done | bytes 262176 | tf_op jit(solution)/shard_map/ppermute | solution.py:36
  67.2 2.3 convolution_add_fusion.11
  69.6 2.3 convolution_add_fusion.10
  71.9 3.4 %collective-permute-done.5 = bf16[4,64,512]{2,1,0:T(8,128)(2,1)S(1)} collective-permute-done((bf16[4,64,512]{2,1,0:T(8,128)(2,1)S(1)}, bf16[4,64,512]{2,1,0:T(8,128)(2,1)S(1)}, u32[]{:S(2)}, u32[]{:S(2)}) %collective-permute-start.5) | collective-permute-done | bytes 262176 | tf_op jit(solution)/shard_map/ppermute | solution.py:36
  75.3 2.3 convolution_add_fusion.9
  78.8 11.8 %psum.106 = f32[512]{0:T(512)S(1)} all-reduce(f32[512]{0:T(512)S(1)} %get-tuple-element.42), channel_id=1, replica_groups=mesh['agent'=8,'res'=4] {'agent'}, use_global_device_ids=true, to_apply=%region_5.6 | all-reduce | flops 512 | bytes 4096 | tf_op jit(solution)/shard_map/psum | solution.py:53
  92.5 9.9 %collective-permute-done.6 = bf16[4,64,512]{2,1,0:T(8,128)(2,1)S(1)} collective-permute-done((bf16[4,64,512]{2,1,0:T(8,128)(2,1)S(1)}, bf16[4,64,512]{2,1,0:T(8,128)(2,1)S(1)}, u32[]{:S(2)}, u32[]{:S(2)}) %collective-permute-start.6) | collective-permute-done | bytes 262176 | tf_op jit(solution)/shard_map/ppermute | solution.py:36
  102.4 2.3 fusion.19
  104.8 6.7 %collective-permute-done.7 = bf16[4,64,512]{2,1,0:T(8,128)(2,1)S(1)} collective-permute-done((bf16[4,64,512]{2,1,0:T(8,128)(2,1)S(1)}, bf16[4,64,512]{2,1,0:T(8,128)(2,1)S(1)}, u32[]{:S(2)}, u32[]{:S(2)}) %collective-permute-start.7) | collective-permute-done | bytes 262176 | tf_op jit(solution)/shard_map/ppermute | solution.py:36
  111.4 2.3 convolution_add_fusion.8
  113.8 2.3 convolution_add_fusion.7
  116.1 3.5 %collective-permute-done.8 = bf16[4,64,512]{2,1,0:T(8,128)(2,1)S(1)} collective-permute-done((bf16[4,64,512]{2,1,0:T(8,128)(2,1)S(1)}, bf16[4,64,512]{2,1,0:T(8,128)(2,1)S(1)}, u32[]{:S(2)}, u32[]{:S(2)}) %collective-permute-start.8) | collective-permute-done | bytes 262176 | tf_op jit(solution)/shard_map/ppermute | solution.py:36
  119.6 2.3 convolution_add_fusion.6
  123.0 11.8 %psum.107 = f32[512]{0:T(512)S(1)} all-reduce(f32[512]{0:T(512)S(1)} %get-tuple-element.40), channel_id=1, replica_groups=mesh['agent'=8,'res'=4] {'agent'}, use_global_device_ids=true, to_apply=%region_7.8 | all-reduce | flops 512 | bytes 4096 | tf_op jit(solution)/shard_map/psum | solution.py:53
  136.8 9.9 %collective-permute-done.9 = bf16[4,64,512]{2,1,0:T(8,128)(2,1)S(1)} collective-permute-done((bf16[4,64,512]{2,1,0:T(8,128)(2,1)S(1)}, bf16[4,64,512]{2,1,0:T(8,128)(2,1)S(1)}, u32[]{:S(2)}, u32[]{:S(2)}) %collective-permute-start.9) | collective-permute-done | bytes 262176 | tf_op jit(solution)/shard_map/ppermute | solution.py:36
  146.7 2.3 fusion.17
  149.0 6.7 %collective-permute-done.10 = bf16[4,64,512]{2,1,0:T(8,128)(2,1)S(1)} collective-permute-done((bf16[4,64,512]{2,1,0:T(8,128)(2,1)S(1)}, bf16[4,64,512]{2,1,0:T(8,128)(2,1)S(1)}, u32[]{:S(2)}, u32[]{:S(2)}) %collective-permute-start.10) | collective-permute-done | bytes 262176 | tf_op jit(solution)/shard_map/ppermute | solution.py:36
  155.7 2.3 convolution_add_fusion.5
  158.0 2.4 convolution_add_fusion.4
  160.4 3.5 %collective-permute-done.11 = bf16[4,64,512]{2,1,0:T(8,128)(2,1)S(1)} collective-permute-done((bf16[4,64,512]{2,1,0:T(8,128)(2,1)S(1)}, bf16[4,64,512]{2,1,0:T(8,128)(2,1)S(1)}, u32[]{:S(2)}, u32[]{:S(2)}) %collective-permute-start.11) | collective-permute-done | bytes 262176 | tf_op jit(solution)/shard_map/ppermute | solution.py:36
  163.8 2.3 convolution_add_fusion.3
  166.2 1.8 gather_fusion.7
  169.1 11.8 %psum.108 = f32[512]{0:T(512)S(1)} all-reduce(f32[512]{0:T(512)S(1)} %get-tuple-element.38), channel_id=1, replica_groups=mesh['agent'=8,'res'=4] {'agent'}, use_global_device_ids=true, to_apply=%region_9.10 | all-reduce | flops 512 | bytes 4096 | tf_op jit(solution)/shard_map/psum | solution.py:53
  182.9 9.9 %collective-permute-done.12 = bf16[4,64,512]{2,1,0:T(8,128)(2,1)S(1)} collective-permute-done((bf16[4,64,512]{2,1,0:T(8,128)(2,1)S(1)}, bf16[4,64,512]{2,1,0:T(8,128)(2,1)S(1)}, u32[]{:S(2)}, u32[]{:S(2)}) %collective-permute-start.12) | collective-permute-done | bytes 262176 | tf_op jit(solution)/shard_map/ppermute | solution.py:36
  195.4 2.4 fusion.15
  197.8 4.1 %collective-permute-done.13 = bf16[4,64,512]{2,1,0:T(8,128)(2,1)} collective-permute-done((bf16[4,64,512]{2,1,0:T(8,128)(2,1)S(1)}, bf16[4,64,512]{2,1,0:T(8,128)(2,1)}, u32[]{:S(2)}, u32[]{:S(2)}) %collective-permute-start.13) | collective-permute-done | bytes 262176 | tf_op jit(solution)/shard_map/ppermute | solution.py:36
  201.9 2.3 convolution_add_fusion.2
  204.2 2.5 convolution_add_fusion.1
  206.7 3.6 %collective-permute-done.14 = bf16[4,64,512]{2,1,0:T(8,128)(2,1)S(1)} collective-permute-done((bf16[4,64,512]{2,1,0:T(8,128)(2,1)}, bf16[4,64,512]{2,1,0:T(8,128)(2,1)S(1)}, u32[]{:S(2)}, u32[]{:S(2)}) %collective-permute-start.14) | collective-permute-done | bytes 262176 | tf_op jit(solution)/shard_map/ppermute | solution.py:36
  210.2 2.3 convolution_add_fusion
  212.6 1.8 gather_fusion.9
  214.3 2.8 multiply_reduce_fusion
  217.2 43.0 %all-reduce = (f32[]{:T(128)}, f32[]{:T(128)}, f32[]{:T(128)}, f32[]{:T(128)}, f32[]{:T(128)}) all-reduce(f32[]{:T(128)} %get-tuple-element.13, f32[]{:T(128)} %get-tuple-element.12, f32[]{:T(128)} %get-tuple-element.11, f32[]{:T(128)} %get-tuple-element.10, f32[]{:T(128)} %get-tuple-element.9), channel_id=1, replica_groups=mesh['agent'=8,'res'=4] {'agent','res'}, use_global_device_ids=true, to_apply=%region_23.24 | all-reduce | flops 5 | bytes 40 | tf_op jit(solution)/shard_map/psum | solution.py:54
  263.5 11.8 %psum.109 = f32[512]{0:T(512)S(1)} all-reduce(f32[512]{0:T(512)S(1)} %get-tuple-element.14), channel_id=1, replica_groups=mesh['agent'=8,'res'=4] {'agent'}, use_global_device_ids=true, to_apply=%region_11.12 | all-reduce | flops 512 | bytes 4096 | tf_op jit(solution)/shard_map/psum | solution.py:53
  276.6 8.7 %all-reduce.1 = (f32[]{:T(128)}, f32[]{:T(128)}, f32[]{:T(128)}, f32[]{:T(128)}, f32[]{:T(128)}) all-reduce(f32[]{:T(128)S(6)} %mul.131, f32[]{:T(128)S(6)} %mul.132, f32[]{:T(128)S(6)} %mul.133, f32[]{:T(128)S(6)} %mul.134, f32[]{:T(128)S(6)} %mul.135), channel_id=1, replica_groups=mesh['agent'=8,'res'=4] {'res'}, use_global_device_ids=true, to_apply=%region_13.14 | all-reduce | flops 5 | bytes 40 | tf_op jit(solution)/shard_map/psum | solution.py:58
  (61 shorter events, 20.6 us)
Async XLA Ops:
  6.7 8.1 %collective-permute-start = (bf16[4,64,512]{2,1,0:T(8,128)(2,1)S(1)}, bf16[4,64,512]{2,1,0:T(8,128)(2,1)S(1)}, u32[]{:S(2)}, u32[]{:S(2)}) collective-permute-start(bf16[4,64,512]{2,1,0:T(8,128)(2,1)S(1)} %bitcast.62), channel_id=1, source_target_pairs={{0,1},{1,2},{2,3},{3,0},{4,5},{5,6},{6,7},{7,4},{8,9},{9,10},{10,1... | collective-permute-start | bytes 786440 | tf_op jit(solution)/shard_map/ppermute | solution.py:36
  14.8 7.8 %collective-permute-start.1 = (bf16[4,64,512]{2,1,0:T(8,128)(2,1)S(1)}, bf16[4,64,512]{2,1,0:T(8,128)(2,1)S(1)}, u32[]{:S(2)}, u32[]{:S(2)}) collective-permute-start(bf16[4,64,512]{2,1,0:T(8,128)(2,1)S(1)} %collective-permute-done), channel_id=1, source_target_pairs={{0,1},{1,2},{2,3},{3,0},{4,5},{5,6},{6,7},{7,4},{8,9},{9,10},{10,1... | collective-permute-start | bytes 786440 | tf_op jit(solution)/shard_map/ppermute | solution.py:36
  19.6 26.8 %copy-start.2 = (f32[512]{0:T(512)S(1)}, f32[512]{0:T(512)}, u32[]{:S(2)}) copy-start(f32[512]{0:T(512)} %param.10) | copy-start | bytes 6148
  19.6 26.8 %copy-start.4 = (f32[512]{0:T(512)S(1)}, f32[512]{0:T(512)}, u32[]{:S(2)}) copy-start(f32[512]{0:T(512)} %param.11) | copy-start | bytes 6148
  19.6 27.4 %copy-start = (f32[256,512]{1,0:T(8,128)S(1)}, f32[256,512]{1,0:T(8,128)}, u32[]{:S(2)}) copy-start(f32[256,512]{1,0:T(8,128)} %param.6) | copy-start | bytes 1572868
  22.6 8.2 %collective-permute-start.2 = (bf16[4,64,512]{2,1,0:T(8,128)(2,1)S(1)}, bf16[4,64,512]{2,1,0:T(8,128)(2,1)S(1)}, u32[]{:S(2)}, u32[]{:S(2)}) collective-permute-start(bf16[4,64,512]{2,1,0:T(8,128)(2,1)S(1)} %collective-permute-done.1), channel_id=1, source_target_pairs={{0,1},{1,2},{2,3},{3,0},{4,5},{5,6},{6,7},{7,4},{8,9},{9,10},{10,1... | collective-permute-start | bytes 786440 | tf_op jit(solution)/shard_map/ppermute | solution.py:36
  48.3 9.9 %collective-permute-start.3 = (bf16[4,64,512]{2,1,0:T(8,128)(2,1)S(1)}, bf16[4,64,512]{2,1,0:T(8,128)(2,1)S(1)}, u32[]{:S(2)}, u32[]{:S(2)}) collective-permute-start(bf16[4,64,512]{2,1,0:T(8,128)(2,1)S(1)} %bitcast.66), channel_id=1, source_target_pairs={{0,1},{1,2},{2,3},{3,0},{4,5},{5,6},{6,7},{7,4},{8,9},{9,10},{10,1... | collective-permute-start | bytes 786440 | tf_op jit(solution)/shard_map/ppermute | solution.py:36
  58.2 9.0 %collective-permute-start.4 = (bf16[4,64,512]{2,1,0:T(8,128)(2,1)S(1)}, bf16[4,64,512]{2,1,0:T(8,128)(2,1)S(1)}, u32[]{:S(2)}, u32[]{:S(2)}) collective-permute-start(bf16[4,64,512]{2,1,0:T(8,128)(2,1)S(1)} %collective-permute-done.3), channel_id=1, source_target_pairs={{0,1},{1,2},{2,3},{3,0},{4,5},{5,6},{6,7},{7,4},{8,9},{9,10},{10,1... | collective-permute-start | bytes 786440 | tf_op jit(solution)/shard_map/ppermute | solution.py:36
  67.2 8.1 %collective-permute-start.5 = (bf16[4,64,512]{2,1,0:T(8,128)(2,1)S(1)}, bf16[4,64,512]{2,1,0:T(8,128)(2,1)S(1)}, u32[]{:S(2)}, u32[]{:S(2)}) collective-permute-start(bf16[4,64,512]{2,1,0:T(8,128)(2,1)S(1)} %collective-permute-done.4), channel_id=1, source_target_pairs={{0,1},{1,2},{2,3},{3,0},{4,5},{5,6},{6,7},{7,4},{8,9},{9,10},{10,1... | collective-permute-start | bytes 786440 | tf_op jit(solution)/shard_map/ppermute | solution.py:36
  92.5 10.0 %collective-permute-start.6 = (bf16[4,64,512]{2,1,0:T(8,128)(2,1)S(1)}, bf16[4,64,512]{2,1,0:T(8,128)(2,1)S(1)}, u32[]{:S(2)}, u32[]{:S(2)}) collective-permute-start(bf16[4,64,512]{2,1,0:T(8,128)(2,1)S(1)} %bitcast.68), channel_id=1, source_target_pairs={{0,1},{1,2},{2,3},{3,0},{4,5},{5,6},{6,7},{7,4},{8,9},{9,10},{10,1... | collective-permute-start | bytes 786440 | tf_op jit(solution)/shard_map/ppermute | solution.py:36
  102.4 9.0 %collective-permute-start.7 = (bf16[4,64,512]{2,1,0:T(8,128)(2,1)S(1)}, bf16[4,64,512]{2,1,0:T(8,128)(2,1)S(1)}, u32[]{:S(2)}, u32[]{:S(2)}) collective-permute-start(bf16[4,64,512]{2,1,0:T(8,128)(2,1)S(1)} %collective-permute-done.6), channel_id=1, source_target_pairs={{0,1},{1,2},{2,3},{3,0},{4,5},{5,6},{6,7},{7,4},{8,9},{9,10},{10,1... | collective-permute-start | bytes 786440 | tf_op jit(solution)/shard_map/ppermute | solution.py:36
  111.4 8.2 %collective-permute-start.8 = (bf16[4,64,512]{2,1,0:T(8,128)(2,1)S(1)}, bf16[4,64,512]{2,1,0:T(8,128)(2,1)S(1)}, u32[]{:S(2)}, u32[]{:S(2)}) collective-permute-start(bf16[4,64,512]{2,1,0:T(8,128)(2,1)S(1)} %collective-permute-done.7), channel_id=1, source_target_pairs={{0,1},{1,2},{2,3},{3,0},{4,5},{5,6},{6,7},{7,4},{8,9},{9,10},{10,1... | collective-permute-start | bytes 786440 | tf_op jit(solution)/shard_map/ppermute | solution.py:36
  136.7 9.9 %collective-permute-start.9 = (bf16[4,64,512]{2,1,0:T(8,128)(2,1)S(1)}, bf16[4,64,512]{2,1,0:T(8,128)(2,1)S(1)}, u32[]{:S(2)}, u32[]{:S(2)}) collective-permute-start(bf16[4,64,512]{2,1,0:T(8,128)(2,1)S(1)} %bitcast.70), channel_id=1, source_target_pairs={{0,1},{1,2},{2,3},{3,0},{4,5},{5,6},{6,7},{7,4},{8,9},{9,10},{10,1... | collective-permute-start | bytes 786440 | tf_op jit(solution)/shard_map/ppermute | solution.py:36
  146.7 9.0 %collective-permute-start.10 = (bf16[4,64,512]{2,1,0:T(8,128)(2,1)S(1)}, bf16[4,64,512]{2,1,0:T(8,128)(2,1)S(1)}, u32[]{:S(2)}, u32[]{:S(2)}) collective-permute-start(bf16[4,64,512]{2,1,0:T(8,128)(2,1)S(1)} %collective-permute-done.9), channel_id=1, source_target_pairs={{0,1},{1,2},{2,3},{3,0},{4,5},{5,6},{6,7},{7,4},{8,9},{9,10},{10,1... | collective-permute-start | bytes 786440 | tf_op jit(solution)/shard_map/ppermute | solution.py:36
  155.7 8.2 %collective-permute-start.11 = (bf16[4,64,512]{2,1,0:T(8,128)(2,1)S(1)}, bf16[4,64,512]{2,1,0:T(8,128)(2,1)S(1)}, u32[]{:S(2)}, u32[]{:S(2)}) collective-permute-start(bf16[4,64,512]{2,1,0:T(8,128)(2,1)S(1)} %collective-permute-done.10), channel_id=1, source_target_pairs={{0,1},{1,2},{2,3},{3,0},{4,5},{5,6},{6,7},{7,4},{8,9},{9,10},{10,1... | collective-permute-start | bytes 786440 | tf_op jit(solution)/shard_map/ppermute | solution.py:36
  182.8 11.9 %copy-start.1 = (bf16[256,512]{1,0:T(8,128)(2,1)}, bf16[256,512]{1,0:T(8,128)(2,1)S(1)}, u32[]{:S(2)}) copy-start(bf16[256,512]{1,0:T(8,128)(2,1)S(1)} %gather_fusion.8) | copy-start | bytes 786436
  182.8 9.9 %collective-permute-start.12 = (bf16[4,64,512]{2,1,0:T(8,128)(2,1)S(1)}, bf16[4,64,512]{2,1,0:T(8,128)(2,1)S(1)}, u32[]{:S(2)}, u32[]{:S(2)}) collective-permute-start(bf16[4,64,512]{2,1,0:T(8,128)(2,1)S(1)} %bitcast.64), channel_id=1, source_target_pairs={{0,1},{1,2},{2,3},{3,0},{4,5},{5,6},{6,7},{7,4},{8,9},{9,10},{10,1... | collective-permute-start | bytes 786440 | tf_op jit(solution)/shard_map/ppermute | solution.py:36
  192.7 9.1 %collective-permute-start.13 = (bf16[4,64,512]{2,1,0:T(8,128)(2,1)S(1)}, bf16[4,64,512]{2,1,0:T(8,128)(2,1)}, u32[]{:S(2)}, u32[]{:S(2)}) collective-permute-start(bf16[4,64,512]{2,1,0:T(8,128)(2,1)S(1)} %collective-permute-done.12), channel_id=1, source_target_pairs={{0,1},{1,2},{2,3},{3,0},{4,5},{5,6},{6,7},{7,4},{8,9},{9,10},{10,1... | collective-permute-start | bytes 786440 | tf_op jit(solution)/shard_map/ppermute | solution.py:36
  201.9 8.4 %collective-permute-start.14 = (bf16[4,64,512]{2,1,0:T(8,128)(2,1)}, bf16[4,64,512]{2,1,0:T(8,128)(2,1)S(1)}, u32[]{:S(2)}, u32[]{:S(2)}) collective-permute-start(bf16[4,64,512]{2,1,0:T(8,128)(2,1)} %collective-permute-done.13), channel_id=1, source_target_pairs={{0,1},{1,2},{2,3},{3,0},{4,5},{5,6},{6,7},{7,4},{8,9},{9,10},{10,1... | collective-permute-start | bytes 786440 | tf_op jit(solution)/shard_map/ppermute | solution.py:36
  275.9 14.5 %copy-start.3 = (f32[512]{0:T(512)}, f32[512]{0:T(512)S(1)}, u32[]{:S(2)}) copy-start(f32[512]{0:T(512)S(1)} %get-tuple-element.26) | copy-start | bytes 6148
